TPU v7x, 256 devices: a whole 4x4x8 slice. The times are simulated.
256 devices in a mesh: dp: 128 (over y, z, x), grp: 2 (over core).
Axes of the slice: x: 4, y: 4, z: 8, core: 2. Of those that a mesh axis runs over, the one named last changes fastest.
Arguments:
- embeddings: bfloat16 [65536, 1024], P(('dp', 'grp')), may hold values from -6 to 6
- owner_dest: int32 [65536, 1], P(('dp', 'grp')), may hold values from 0 to 127; in each aligned block of 256 rows (0 to 255, 256 to 511, ...) at most 6 rows name the same one
- cluster_slot: int32 [65536, 1], P(('dp', 'grp')), may hold values from 0 to 7
- cluster_rank: int32 [1024], replicated, may hold values from 0 to 1023, each once
- centroids: bfloat16 [1024, 1024], P('dp'), may hold values from -2 to 2
Outputs:
- shift: bfloat16 [1024, 1792], replicated
- moment: float32 [1024, 256, 256], P(('dp', 'grp'))
Inputs may be any that keep to these rules, and one draw needn't show every extreme that they name: `owner_dest`: among the rows of one device (aligned blocks of 256 rows), no owner is named by more than 6 rows, a bound that some block reaches. `cluster_rank`: A permutation.
All inputs are finite; a program needn't handle non-finite values.
Results may differ from a plain program's by a relative error of at most 0.0034.
Values may be sent and summed in bfloat16 or wider, within the bound.
A program may use at most 64 MiB of HBM per device.

v0:
```python
import jax
import jax.numpy as jnp
from jax import lax
from jax.sharding import PartitionSpec as P

D = 1024
D_SMALL = 256
D_MID = 512


def residuals(rows, cent):
    rows = rows.astype(jnp.float32)
    pieces = []
    for width in (D_SMALL, D_MID, D):
        part = rows[:, :width]
        scale = lax.rsqrt(jnp.mean(part * part, axis=-1, keepdims=True) + 1e-06)
        pieces.append(part * scale - cent[:, :width])
    return jnp.concatenate(pieces, axis=1).astype(jnp.bfloat16)


def slot_onehot(slots, per_owner):
    return (slots[:, None] == jnp.arange(per_owner, dtype=jnp.int32)[None, :]).astype(jnp.bfloat16)


def moments(select, small):
    count_rows = small.shape[0]
    per_owner = select.shape[1]
    spread = (select[:, :, None] * small[:, None, :]).reshape(count_rows, per_owner * D_SMALL)
    gram = jnp.einsum("sa,sb->ab", spread, small, preferred_element_type=jnp.float32)
    return gram.reshape(per_owner, D_SMALL, D_SMALL)


def on_device(embeddings, owner_dest, cluster_slot, cluster_rank, centroids):
    rows_here = embeddings.shape[0]
    width = embeddings.shape[1]
    owners = lax.axis_size("dp")
    per_owner = centroids.shape[0]
    capacity = 3 * rows_here // owners
    dest = owner_dest[:, 0]
    slot = cluster_slot[:, 0]
    hits = (dest[:, None] == jnp.arange(owners, dtype=jnp.int32)[None, :]).astype(jnp.int32)
    before = jnp.cumsum(hits, axis=0) - hits
    position = jnp.sum(before * hits, axis=1)
    target = dest * capacity + position

    def pack(values, fill):
        buffer = jnp.full((owners * capacity,) + values.shape[1:], fill, values.dtype)
        buffer = buffer.at[target].set(values)
        return buffer.reshape((owners, capacity) + values.shape[1:])

    sent_ids = pack(slot, -1)
    sent_rows = pack(embeddings, 0)
    got_rows = lax.all_to_all(sent_rows, "dp", split_axis=0, concat_axis=0, tiled=True)
    got_ids = lax.all_to_all(sent_ids, "dp", split_axis=0, concat_axis=0, tiled=True)
    lead = got_rows.shape[0]
    middle = got_rows.shape[1]
    flat_ids = got_ids.reshape(-1)
    select = slot_onehot(flat_ids, per_owner)
    cent = jnp.dot(select, centroids, preferred_element_type=jnp.float32)
    resid = residuals(got_rows.reshape(-1, width), cent)
    resid, got_ids = (resid.reshape(lead, middle, resid.shape[1]), got_ids)
    resid = resid.reshape(-1, resid.shape[2])
    select = slot_onehot(got_ids.reshape(-1), per_owner)
    sums = jnp.einsum("sc,sw->cw", select, resid, preferred_element_type=jnp.float32)
    counts = jnp.sum(select.astype(jnp.float32), axis=0)
    gram = moments(select, resid[:, :D_SMALL])
    sums_part, counts_part, gram_part = (
        lax.psum_scatter(sums, "grp", scatter_dimension=0, tiled=True),
        lax.psum_scatter(counts, "grp", scatter_dimension=0, tiled=True),
        lax.psum_scatter(gram, "grp", scatter_dimension=0, tiled=True),
    )
    denom = counts_part + 1.0
    table_part = (sums_part / denom[:, None]).astype(jnp.bfloat16)
    table = lax.all_gather(table_part, ("dp", "grp"), axis=0, tiled=True)
    shift = table[cluster_rank]
    moment = gram_part / denom[:, None, None]
    return (shift, moment)


def solution(mesh):
    placed = (
        P(("dp", "grp"), None),
        P(("dp", "grp"), None),
        P(("dp", "grp"), None),
        P(),
        P("dp", None),
    )
    return jax.shard_map(
        on_device,
        mesh=mesh,
        in_specs=placed,
        out_specs=(P(), P(("dp", "grp"), None, None)),
        check_vma=False,
    )
```

profile of v0, /device:TPU:1, one launch (start us, length us, event | category | flops | bytes accessed | tf_op | source)
XLA Modules:
  0.0 256.8 jit_solution(13013240612006386319)
XLA Ops:
  8.0 0.0 copy-start
  8.0 0.8 copy.12
  8.8 0.2 fusion.16
  9.1 0.9 fusion.18
  10.0 0.7 compare_select_fusion.1
  10.7 1.6 scatter_custom_fusion
  12.2 0.8 all_to_all.9
  13.0 16.3 %all-to-all-start = ((s32[128,1,6]{2,1,0:T(1,128)}), s32[128,1,6]{2,1,0:T(1,128)S(1)}, u32[]{:S(2)}, u32[]{:S(2)}) async-start(s32[128,1,6]{2,1,0:T(1,128)} %bitcast.8), calls=%async_computation | async-start | bytes 131072 | tf_op jit(solution)/shard_map/all_to_all | solution.py:54
  29.3 2.6 %scatter_custom_fusion.1 = bf16[768,1024]{1,0:T(8,128)(2,1)S(1)} fusion(s32[256]{0:T(256)S(1)} %bitcast.40, bf16[256,1024]{1,0:T(8,128)(2,1)} %param.5, bf16[]{:T(256)} %constant.7.clone.1), kind=kCustom, calls=%fused_computation.22 | custom fusion | bytes 1573376 | tf_op jit(solution)/shard_map/scatter | solution.py:48
  32.0 1.6 reshape.100
  33.5 6.3 %all-to-all-done = s32[128,1,6]{2,1,0:T(1,128)S(1)} async-done(((s32[128,1,6]{2,1,0:T(1,128)}), s32[128,1,6]{2,1,0:T(1,128)S(1)}, u32[]{:S(2)}, u32[]{:S(2)}) %all-to-all-start) | async-done | bytes 3104 | tf_op jit(solution)/shard_map/all_to_all | solution.py:54
  39.8 6.9 %all-to-all-start.1 = ((bf16[128,6,1024]{2,1,0:T(8,128)(2,1)}), bf16[128,6,1024]{2,1,0:T(8,128)(2,1)S(1)}, u32[]{:S(2)}, u32[]{:S(2)}) async-start(bf16[128,6,1024]{2,1,0:T(8,128)(2,1)} %reshape.100), calls=%async_computation.1 | async-start | bytes 4194304 | tf_op jit(solution)/shard_map/all_to_all | solution.py:53
  46.8 0.0 reduce-scatter.2.cloned.1.call-start
  46.8 0.5 broadcast.108
  47.4 0.8 reduce.4
  48.2 0.1 eq.59
  48.3 0.0 copy-start.4
  48.3 0.6 fusion.22
  48.9 47.0 %all-to-all-done.1 = bf16[128,6,1024]{2,1,0:T(8,128)(2,1)S(1)} async-done(((bf16[128,6,1024]{2,1,0:T(8,128)(2,1)}), bf16[128,6,1024]{2,1,0:T(8,128)(2,1)S(1)}, u32[]{:S(2)}, u32[]{:S(2)}) %all-to-all-start.1) | async-done | bytes 1572896 | tf_op jit(solution)/shard_map/all_to_all | solution.py:53
  95.9 0.6 multiply_reduce_fusion
  96.5 0.7 copy-done.1
  97.2 0.1 rsqrt.30
  97.3 2.5 reshape.101
  99.9 0.2 multiply_reduce_fusion.2
  100.1 1.8 subtract_convert_fusion
  101.9 1.7 copy-done.2
  103.6 0.2 fusion.12
  103.7 0.9 copy.15
  104.7 3.3 %fusion = f32[8,256,256]{2,1,0:T(8,128)} fusion(bf16[768,256]{0,1:T(8,128)(2,1)} %copy.15, bf16[768,8]{0,1:T(8,128)(2,1)} %fusion.22, bf16[768,256]{1,0:T(8,128)(2,1)S(1)} %fusion.12), kind=kOutput, calls=%fused_computation.4 | convolution fusion | flops 806879232 | bytes 2895872 | tf_op jit(solution)/shard_map/sa,sb->ab/dot_general | solution.py:29
  108.0 0.0 reduce-scatter.2.cloned.1.call-update
  108.0 0.0 all-gather.3.cloned.1.call-start
  108.1 1.4 dynamic-slice
  109.5 1.3 convert_reduce_fusion
  110.8 0.2 multiply_reduce_fusion.1
  111.0 1.6 fusion.9
  112.6 0.0 copy-done.3
  112.7 0.0 copy-start.7
  112.7 0.0 copy-start.6
  112.7 0.5 fusion.3
  113.8 7.5 %all-reduce.2 = (f32[8]{0:T(128)S(1)}, f32[8,1792]{1,0:T(8,128)S(1)}) all-reduce(f32[8]{0:T(128)S(1)} %copy-done.7, f32[8,1792]{1,0:T(8,128)S(1)} %fusion.3), channel_id=3, replica_groups=mesh['dp'=128,'grp'=2] {'grp'}, use_global_device_ids=true, to_apply=%region_10.11.clone | all-reduce | flops 14344 | bytes 114752
  121.3 0.1 dynamic-slice_add_fusion
  121.4 0.7 fusion.24
  122.1 0.0 all-gather.3.cloned.1.call-update
  122.1 0.0 reduce-scatter.2.cloned.1.call-done
  122.2 2.4 broadcast_divide_fusion
  124.5 107.6 %all-gather.3.cloned.1.call-done = bf16[256,4,1792]{2,1,0:T(4,128)(2,1)} async-done(((bf16[1,4,1792]{2,1,0:T(4,128)(2,1)}), bf16[256,4,1792]{2,1,0:T(4,128)(2,1)}) %all-gather.3.cloned.1.call-update) | async-done | bytes 3670032 | tf_op jit(solution)/shard_map/all_gather | solution.py:74
  232.1 6.9 %reshape.128 = bf16[1024,1792]{1,0:T(8,128)(2,1)} reshape(bf16[256,4,1792]{2,1,0:T(4,128)(2,1)} %all-gather.3.cloned.1.call-done) | data formatting | bytes 7340032
  238.9 10.4 %gather_fusion = bf16[1024,1792]{1,0:T(8,128)(2,1)} fusion(bf16[1024,1792]{1,0:T(8,128)(2,1)} %reshape.128, s32[1024]{0:T(1024)S(1)} %fusion.27), kind=kCustom, calls=%fused_computation | custom fusion | bytes 7344128 | tf_op jit(solution)/shard_map/gather | solution.py:75
  (19 shorter events, 0.1 us)
Async XLA Ops:
  8.0 92.1 %copy-start = (bf16[8,1024]{1,0:T(8,128)(2,1)S(1)}, bf16[8,1024]{1,0:T(8,128)(2,1)}, u32[]{:S(2)}) copy-start(bf16[8,1024]{1,0:T(8,128)(2,1)} %param.9) | copy-start | bytes 49156
  13.0 26.9 %all-to-all-start = ((s32[128,1,6]{2,1,0:T(1,128)}), s32[128,1,6]{2,1,0:T(1,128)S(1)}, u32[]{:S(2)}, u32[]{:S(2)}) async-start(s32[128,1,6]{2,1,0:T(1,128)} %bitcast.8), calls=%async_computation | async-start | bytes 131072 | tf_op jit(solution)/shard_map/all_to_all | solution.py:54
  39.8 56.0 %all-to-all-start.1 = ((bf16[128,6,1024]{2,1,0:T(8,128)(2,1)}), bf16[128,6,1024]{2,1,0:T(8,128)(2,1)S(1)}, u32[]{:S(2)}, u32[]{:S(2)}) async-start(bf16[128,6,1024]{2,1,0:T(8,128)(2,1)} %reshape.100), calls=%async_computation.1 | async-start | bytes 4194304 | tf_op jit(solution)/shard_map/all_to_all | solution.py:53
  46.8 75.4 %reduce-scatter.2.cloned.1.call-start = ((), (), s32[]{:S(2)}) async-start(), calls=%async_computation.3 | async-start | bytes 3145728 | tf_op jit(solution)/shard_map/reduce_scatter | solution.py:70
  48.3 51.8 %copy-start.4 = (s32[768]{0:T(1024)}, s32[768]{0:T(1024)S(1)}, u32[]{:S(2)}) copy-start(s32[768]{0:T(1024)S(1)} %eq.59) | copy-start | bytes 9220
  95.9 1.3 copy-start.1
  101.9 1.7 copy-start.2
  108.0 124.1 %all-gather.3.cloned.1.call-start = ((), (), s32[]{:S(2)}) async-start(), calls=%async_computation.4 | async-start | bytes 3684352 | tf_op jit(solution)/shard_map/all_gather | solution.py:74
  108.1 4.6 %copy-start.3 = (bf16[768,1024]{1,0:T(8,128)(2,1)S(1)}, bf16[768,1024]{1,0:T(8,128)(2,1)}, u32[]{:S(2)}) copy-start(bf16[768,1024]{1,0:T(8,128)(2,1)} %get-tuple-element.4) | copy-start | bytes 4718596
  108.1 4.6 %copy-start.5 = (s32[768]{0:T(1024)S(1)}, s32[768]{0:T(1024)}, u32[]{:S(2)}) copy-start(s32[768]{0:T(1024)} %copy-done.4) | copy-start | bytes 9220
  112.7 1.1 copy-start.7
  112.7 9.5 %copy-start.6 = (s32[1024]{0:T(1024)S(1)}, s32[1024]{0:T(1024)}, u32[]{:S(2)}) copy-start(s32[1024]{0:T(1024)} %param.8) | copy-start | bytes 12292
Sparse Core Ops, SparseCore 0:
  108.1 13.3 reduce-scatter.1
Sparse Core Ops, SparseCore 1:
  122.2 109.8 all-gather.2
where the time goes:
time: 258 us; the launch traced here: 257 us
  waiting for transfers between devices  161 us (62%)
  local copies, waits for them, and re-layouts  32.7 us (13%)
  starting transfers between devices  23.4 us (9%)
  between operations  16.4 us (6%)
  other arithmetic  10.4 us (4%)
  blocking collectives  7.53 us (3%)
  matrix products  5.58 us (2%)
    all_gather x1, waiting for transfers between devices, on_device(): table = lax.all_gather(table_part, ('dp', 'grp'), axis=0, tiled=True)  108 us
    all_to_all x1, waiting for transfers between devices, on_device(): lax.all_to_all(sent_rows, 'dp', split_axis=0, concat_axis=0, tiled=True)  47 us
    all_to_all x1, starting transfers between devices, on_device(): lax.all_to_all(sent_ids, 'dp', split_axis=0, concat_axis=0, tiled=True)  16.3 us
    unnamed x19, local copies, waits for them, and re-layouts  10.7 us
    gather x1, local copies, waits for them, and re-layouts, on_device(): shift = table[cluster_rank]  10.4 us
    unnamed x1, blocking collectives  7.53 us
    all_to_all x1, starting transfers between devices, on_device(): lax.all_to_all(sent_rows, 'dp', split_axis=0, concat_axis=0, tiled=True)  6.94 us
    all_to_all x1, waiting for transfers between devices, on_device(): lax.all_to_all(sent_ids, 'dp', split_axis=0, concat_axis=0, tiled=True)  6.3 us
  transfers between devices with their start and end apart: 4, of which 3 were waited for; matrix products, arithmetic and copies ran while one was open for 6% of the time, Pallas kernels for 0%

commit v1 on v0

--- a/solution.py
+++ b/solution.py
@@ -71,7 +71,10 @@
     )
     denom = counts_part + 1.0
     table_part = (sums_part / denom[:, None]).astype(jnp.bfloat16)
-    table = lax.all_gather(table_part, ("dp", "grp"), axis=0, tiled=True)
+    table = jnp.concatenate(
+        lax.all_to_all(jnp.stack([table_part] * lax.axis_size(("dp", "grp"))), ("dp", "grp"), 0, 0),
+        axis=0,
+    )
     shift = table[cluster_rank]
     moment = gram_part / denom[:, None, None]
     return (shift, moment)

time: 258 us -> 231 us (0.90)
  waiting for transfers between devices: 161 us -> 133 us
  starting transfers between devices: 23.4 us -> 30.9 us
    all_gather x1 -> x0, waiting for transfers between devices: 108 us -> none  [on_device(): table = lax.all_gather(table_part, ('dp', 'grp'), axis=0, tiled=True)]
    all_to_all x0 -> x1, waiting for transfers between devices: none -> 63.3 us  [on_device(): lax.all_to_all(jnp.stack([table_part] * lax.axis_size(('dp', 'grp'))), ('...]
    reduce_scatter x1, waiting for transfers between devices: 0.02 us -> 18 us  [on_device(): lax.psum_scatter(gram, 'grp', scatter_dimension=0, tiled=True)]
    unnamed x19 -> x16, local copies, waits for them, and re-layouts: 10.7 us -> 0.95 us
    all_to_all x0 -> x1, starting transfers between devices: none -> 7.05 us  [on_device(): lax.all_to_all(jnp.stack([table_part] * lax.axis_size(('dp', 'grp'))), ('...]
    reshape x0 -> x1, local copies, waits for them, and re-layouts: none -> 6.87 us  [on_device(): jnp.concatenate(lax.all_to_all(jnp.stack([table_part] * lax.axis_size(('d...]
    another operation x3 -> x4, local copies, waits for them, and re-layouts: 0.02 us -> 2.81 us  [the longest x1 2.79 us: on_device(): jnp.stack([table_part] * lax.axis_size(('dp', 'grp')))]
  transfers between devices with their start and end apart: 4 -> 4, of which waited for: 3 -> 4; matrix products, arithmetic and copies ran while one was open for 6% -> 5% of each run, Pallas kernels for 0% -> 0%
where the time goes in v1:
time: 231 us; the launch traced here: 230 us
  waiting for transfers between devices  133 us (58%)
  local copies, waits for them, and re-layouts  31.9 us (14%)
  starting transfers between devices  30.9 us (13%)
  between operations  14.9 us (6%)
  other arithmetic  8.84 us (4%)
  blocking collectives  7.79 us (3%)
  matrix products  3.43 us (1%)
    all_to_all x1, waiting for transfers between devices, on_device(): lax.all_to_all(jnp.stack([table_part] * lax.axis_size(('dp', 'grp'))), ('...  63.3 us
    all_to_all x1, waiting for transfers between devices, on_device(): lax.all_to_all(sent_rows, 'dp', split_axis=0, concat_axis=0, tiled=True)  45.1 us
    reduce_scatter x1, waiting for transfers between devices, on_device(): lax.psum_scatter(gram, 'grp', scatter_dimension=0, tiled=True)  18 us
    all_to_all x1, starting transfers between devices, on_device(): lax.all_to_all(sent_ids, 'dp', split_axis=0, concat_axis=0, tiled=True)  16.3 us
    gather x1, local copies, waits for them, and re-layouts, on_device(): shift = table[cluster_rank]  10.4 us
    unnamed x1, blocking collectives  7.79 us
    all_to_all x1, starting transfers between devices, on_device(): lax.all_to_all(sent_rows, 'dp', split_axis=0, concat_axis=0, tiled=True)  7.49 us
    all_to_all x1, starting transfers between devices, on_device(): lax.all_to_all(jnp.stack([table_part] * lax.axis_size(('dp', 'grp'))), ('...  7.05 us
  transfers between devices with their start and end apart: 4, of which 4 were waited for; matrix products, arithmetic and copies ran while one was open for 5% of the time, Pallas kernels for 0%

profile of v1, /device:TPU:1, one launch (start us, length us, event | category | flops | bytes accessed | tf_op | source)
XLA Modules:
  0.0 230.5 jit_solution(12737741194910523419)
XLA Ops:
  7.2 0.0 copy-start
  7.2 0.8 copy.12
  8.0 0.2 fusion.16
  8.3 0.9 fusion.18
  9.1 0.7 compare_select_fusion.1
  9.8 1.6 scatter_custom_fusion
  11.4 0.8 all_to_all.12
  12.2 16.3 %all-to-all-start = ((s32[128,1,6]{2,1,0:T(1,128)}), s32[128,1,6]{2,1,0:T(1,128)S(1)}, u32[]{:S(2)}, u32[]{:S(2)}) async-start(s32[128,1,6]{2,1,0:T(1,128)} %bitcast.8), calls=%async_computation | async-start | bytes 131072 | tf_op jit(solution)/shard_map/all_to_all | solution.py:54
  28.5 2.6 %scatter_custom_fusion.1 = bf16[768,1024]{1,0:T(8,128)(2,1)S(1)} fusion(s32[256]{0:T(256)S(1)} %bitcast.38, bf16[256,1024]{1,0:T(8,128)(2,1)} %param.5, bf16[]{:T(256)} %constant.7.clone.1), kind=kCustom, calls=%fused_computation.22 | custom fusion | bytes 1573376 | tf_op jit(solution)/shard_map/scatter | solution.py:48
  31.1 0.0 copy-start.6
  31.1 1.6 reshape.105
  32.7 6.3 %all-to-all-done = s32[128,1,6]{2,1,0:T(1,128)S(1)} async-done(((s32[128,1,6]{2,1,0:T(1,128)}), s32[128,1,6]{2,1,0:T(1,128)S(1)}, u32[]{:S(2)}, u32[]{:S(2)}) %all-to-all-start) | async-done | bytes 3104 | tf_op jit(solution)/shard_map/all_to_all | solution.py:54
  39.0 7.5 %all-to-all-start.1 = ((bf16[128,6,1024]{2,1,0:T(8,128)(2,1)}), bf16[128,6,1024]{2,1,0:T(8,128)(2,1)}, u32[]{:S(2)}, u32[]{:S(2)}) async-start(bf16[128,6,1024]{2,1,0:T(8,128)(2,1)} %reshape.105), calls=%async_computation.1 | async-start | bytes 4194304 | tf_op jit(solution)/shard_map/all_to_all | solution.py:53
  46.5 0.0 copy-done.6
  46.5 0.6 dynamic-slice
  47.8 0.5 broadcast.110
  48.3 0.8 reduce.4
  49.1 0.1 eq.59
  49.2 0.0 copy-start.1
  49.2 0.6 convert_reduce_fusion
  49.9 45.1 %all-to-all-done.1 = bf16[128,6,1024]{2,1,0:T(8,128)(2,1)} async-done(((bf16[128,6,1024]{2,1,0:T(8,128)(2,1)}), bf16[128,6,1024]{2,1,0:T(8,128)(2,1)}, u32[]{:S(2)}, u32[]{:S(2)}) %all-to-all-start.1) | async-done | bytes 1572896 | tf_op jit(solution)/shard_map/all_to_all | solution.py:53
  95.0 2.5 %reshape.107 = f32[768,1024]{1,0:T(8,128)S(1)} reshape(bf16[128,6,1024]{2,1,0:T(8,128)(2,1)} %all-to-all-done.1) | data formatting | bytes 4718592 | tf_op jit(solution)/shard_map/convert_element_type | solution.py:12
  97.5 0.2 multiply_reduce_fusion.1
  97.7 0.2 multiply_reduce_fusion.2
  97.9 2.2 multiply_reduce_fusion
  100.1 0.1 rsqrt.30
  100.3 0.6 subtract_convert_fusion
  100.9 0.0 copy-start.2
  100.9 0.3 fusion.9
  101.2 0.2 fusion.12
  101.4 0.2 copy-done.2
  101.6 0.5 fusion.3
  102.1 0.1 copy-done.5
  102.2 7.8 %all-reduce.2 = (f32[8,1792]{1,0:T(8,128)S(1)}, f32[8]{0:T(128)S(1)}) all-reduce(f32[8,1792]{1,0:T(8,128)S(1)} %fusion.3, f32[8]{0:T(128)S(1)} %copy-done.5), channel_id=2, replica_groups=mesh['dp'=128,'grp'=2] {'grp'}, use_global_device_ids=true, to_apply=%region_8.9.clone | all-reduce | flops 14344 | bytes 114752
  110.0 0.1 dynamic-slice_add_fusion
  110.1 0.1 fusion.21
  110.2 2.8 %stack.2 = bf16[256,4,1792]{2,1,0:T(4,128)(2,1)} broadcast(bf16[4,1792]{1,0:T(4,128)(2,1)S(1)} %fusion.21), dimensions={1,2} | broadcast | bytes 3684352 | tf_op jit(solution)/shard_map/stack | solution.py:75
  113.0 7.1 %all-to-all-start.2 = ((bf16[256,4,1792]{2,1,0:T(4,128)(2,1)}), bf16[256,4,1792]{2,1,0:T(4,128)(2,1)}, u32[]{:S(2)}, u32[]{:S(2)}) async-start(bf16[256,4,1792]{2,1,0:T(4,128)(2,1)} %stack.2), calls=%async_computation.2 | async-start | bytes 7340032 | tf_op jit(solution)/shard_map/all_to_all | solution.py:75
  120.0 0.0 reduce-scatter.2.cloned.1.call-start
  120.1 0.2 copy.15
  120.3 0.0 copy-start.4
  120.3 2.3 %fusion = f32[8,256,256]{2,1,0:T(8,128)} fusion(bf16[768,256]{0,1:T(8,128)(2,1)S(1)} %copy.15, bf16[768,8]{0,1:T(8,128)(2,1)S(1)} %fusion.22, bf16[768,256]{1,0:T(8,128)(2,1)S(1)} %fusion.12), kind=kOutput, calls=%fused_computation.4 | convolution fusion | flops 806879232 | bytes 2895872 | tf_op jit(solution)/shard_map/sa,sb->ab/dot_general | solution.py:29
  122.6 0.0 reduce-scatter.2.cloned.1.call-update
  122.7 18.0 %reduce-scatter.2.cloned.1.call-done = f32[4,256,256]{2,1,0:T(8,128)} async-done(((f32[8,256,256]{2,1,0:T(8,128)}), f32[4,256,256]{2,1,0:T(8,128)}) %reduce-scatter.2.cloned.1.call-update) | async-done | bytes 1048592 | tf_op jit(solution)/shard_map/reduce_scatter | solution.py:70
  140.7 2.4 %broadcast_divide_fusion = f32[4,256,256]{2,1,0:T(8,128)} fusion(f32[4,256,256]{2,1,0:T(8,128)} %reduce-scatter.2.cloned.1.call-done, f32[4]{0:T(128)S(1)} %dynamic-slice_add_fusion), kind=kLoop, calls=%fused_computation.24 | loop fusion | flops 262144 | bytes 2097168 | tf_op jit(solution)/shard_map/div | solution.py:79
  143.0 63.3 %all-to-all-done.2 = bf16[256,4,1792]{2,1,0:T(4,128)(2,1)} async-done(((bf16[256,4,1792]{2,1,0:T(4,128)(2,1)}), bf16[256,4,1792]{2,1,0:T(4,128)(2,1)}, u32[]{:S(2)}, u32[]{:S(2)}) %all-to-all-start.2) | async-done | bytes 3670048 | tf_op jit(solution)/shard_map/all_to_all | solution.py:75
  206.3 6.9 %reshape.106 = bf16[1024,1792]{1,0:T(8,128)(2,1)} reshape(bf16[256,4,1792]{2,1,0:T(4,128)(2,1)} %all-to-all-done.2) | data formatting | bytes 7340032 | tf_op jit(solution)/shard_map/reshape | solution.py:74
  213.2 10.4 %gather_fusion = bf16[1024,1792]{1,0:T(8,128)(2,1)} fusion(bf16[1024,1792]{1,0:T(8,128)(2,1)} %reshape.106, s32[1024]{0:T(1024)S(1)} %fusion.26), kind=kCustom, calls=%fused_computation | custom fusion | bytes 7344128 | tf_op jit(solution)/shard_map/gather | solution.py:78
  (17 shorter events, 0.1 us)
Async XLA Ops:
  7.2 93.1 %copy-start = (bf16[8,1024]{1,0:T(8,128)(2,1)S(1)}, bf16[8,1024]{1,0:T(8,128)(2,1)}, u32[]{:S(2)}) copy-start(bf16[8,1024]{1,0:T(8,128)(2,1)} %param.9) | copy-start | bytes 49156
  12.2 26.9 %all-to-all-start = ((s32[128,1,6]{2,1,0:T(1,128)}), s32[128,1,6]{2,1,0:T(1,128)S(1)}, u32[]{:S(2)}, u32[]{:S(2)}) async-start(s32[128,1,6]{2,1,0:T(1,128)} %bitcast.8), calls=%async_computation | async-start | bytes 131072 | tf_op jit(solution)/shard_map/all_to_all | solution.py:54
  31.1 15.4 %copy-start.6 = (u32[256]{0:T(256)S(1)}, u32[256]{0:T(256)}, u32[]{:S(2)}) copy-start(u32[256]{0:T(256)} %constant.36) | copy-start | bytes 3076
  39.0 55.9 %all-to-all-start.1 = ((bf16[128,6,1024]{2,1,0:T(8,128)(2,1)}), bf16[128,6,1024]{2,1,0:T(8,128)(2,1)}, u32[]{:S(2)}, u32[]{:S(2)}) async-start(bf16[128,6,1024]{2,1,0:T(8,128)(2,1)} %reshape.105), calls=%async_computation.1 | async-start | bytes 4194304 | tf_op jit(solution)/shard_map/all_to_all | solution.py:53
  49.2 51.0 %copy-start.1 = (s32[768]{0:T(1024)}, s32[768]{0:T(1024)S(1)}, u32[]{:S(2)}) copy-start(s32[768]{0:T(1024)S(1)} %eq.59) | copy-start | bytes 9220
  100.9 0.7 copy-start.2
  101.6 0.6 copy-start.5
  113.0 7.1 %copy-start.3 = (s32[768]{0:T(1024)S(1)}, s32[768]{0:T(1024)}, u32[]{:S(2)}) copy-start(s32[768]{0:T(1024)} %copy-done.1) | copy-start | bytes 9220
  113.0 93.4 %all-to-all-start.2 = ((bf16[256,4,1792]{2,1,0:T(4,128)(2,1)}), bf16[256,4,1792]{2,1,0:T(4,128)(2,1)}, u32[]{:S(2)}, u32[]{:S(2)}) async-start(bf16[256,4,1792]{2,1,0:T(4,128)(2,1)} %stack.2), calls=%async_computation.2 | async-start | bytes 7340032 | tf_op jit(solution)/shard_map/all_to_all | solution.py:75
  120.0 20.7 %reduce-scatter.2.cloned.1.call-start = ((), (), s32[]{:S(2)}) async-start(), calls=%async_computation.4 | async-start | bytes 3145728 | tf_op jit(solution)/shard_map/reduce_scatter | solution.py:70
  120.3 2.4 %copy-start.4 = (s32[1024]{0:T(1024)S(1)}, s32[1024]{0:T(1024)}, u32[]{:S(2)}) copy-start(s32[1024]{0:T(1024)} %param.8) | copy-start | bytes 12292
Sparse Core Ops, SparseCore 0:
  123.3 17.3 reduce-scatter.1
